TPU v7x, 128 devices: a whole 4x4x4 slice. The times are simulated.
128 devices in a mesh: group: 2 (over y_lo), row: 8 (over x, y_hi), head: 8 (over z, core).
Axes of the slice: x: 4, y: 4 (y_hi: 2, y_lo: 2; y = y_hi * 2 + y_lo), z: 4, core: 2. Of those that a mesh axis runs over, the one named last changes fastest.
Arguments:
- latent: bfloat16 [2048, 3072], P('row', 'head'), may hold values from -6 to 6
- hint: bfloat16 [2048, 3072], P('row', 'head'), may hold values from -6 to 6
- timestep: int32 [1], replicated, may hold values from 0 to 7
- modulation: float32 [2, 8, 3, 3072], P('group'), may hold values from -3 to 3
- qkv_weight: bfloat16 [2, 3, 3072, 3072], P('group', None, None, 'head'), may hold values from -0.109375 to 0.109375
- out_weight: bfloat16 [2, 3072, 3072], P('group', None, 'head'), may hold values from -0.109375 to 0.109375
- zero_weight: bfloat16 [3072, 3072], P(None, 'head'), may hold values from -0.109375 to 0.109375
- cotangent: bfloat16 [2048, 3072], P('row', 'head'), may hold values from -6 to 6
Outputs:
- mixed: bfloat16 [2048, 3072], P('row', 'head')
- latent_grad: float32 [8, 2, 128, 3072], P('row', 'group', None, 'head')
- hint_grad: float32 [8, 2, 128, 3072], P('row', 'group', None, 'head')
- qkv_grad: float32 [3072, 3, 3072], P(('group', 'row'), None, 'head')
- out_grad: float32 [3072, 3072], P(('group', 'row'), 'head')
- zero_grad: float32 [3072, 3072], P(('group', 'row'), 'head')
All inputs are finite; a program needn't handle non-finite values.
Results may differ from a plain program's by a relative error of at most 0.015.
Values may be sent and summed in bfloat16 or wider, within the bound.
No kernel may reach another device: no remote copies, remote signals or barrier semaphores. Data moves between devices by JAX's collectives and lax.ppermute only.
A program may use at most 128 MiB of HBM per device.

v0:
```python
import jax
import jax.numpy as jnp
from jax import lax
from jax.sharding import Mesh
from jax.sharding import PartitionSpec as P

HD = 128
ROW = ("row_0", "row_1")
GROUP_ROW = ("group", "row_0", "row_1")
EPS = 1e-06


def copy_for_each(array, axis):
    copies = jnp.broadcast_to(array, (lax.axis_size(axis), *array.shape))
    return lax.all_to_all(copies, axis, split_axis=0, concat_axis=0, tiled=True)


def in_order(pieces, dim):
    lengths = list(pieces.shape[1:])
    lengths[dim] *= pieces.shape[0]
    return jnp.moveaxis(pieces, 0, dim).reshape(lengths)


def gather_directly(array, axis, dim):
    pieces = copy_for_each(array, axis)
    return in_order(pieces, dim)


def sent_together(arrays, axis, dim, along):
    both = jnp.concatenate(arrays, axis=along)
    filled, at, finished = (lax.all_gather(both, axis, axis=dim, tiled=True), 0, [])
    for a in arrays:
        finished.append(lax.slice_in_dim(filled, at, at + a.shape[along], axis=along))
        at += a.shape[along]
    return tuple(finished)


def in_blocks(array, dim, peers):
    lengths = array.shape
    pieces = array.reshape(*lengths[:dim], peers, lengths[dim] // peers, *lengths[dim + 1 :])
    return jnp.moveaxis(pieces, dim, 0)


def sum_at_owner(array, axis, dim):
    pieces = in_blocks(array, dim, lax.axis_size(axis))
    arrived = lax.all_to_all(pieces, axis, split_axis=0, concat_axis=0, tiled=True)
    return arrived.sum(axis=0)


def from_partner(block, axis, distance):
    count = lax.axis_size(axis)
    route = []
    for low in range(count):
        high = low | 1 << distance
        if high != low and high < count:
            route += [(low, high), (high, low)]
    return lax.ppermute(block, axis, route)


def taken_together(array, axis):
    everything = copy_for_each(array, axis)
    return jnp.sum(everything, axis=0)


def together(arrays, axis):
    ravelled, at, finished = (jnp.concatenate([a.reshape(-1) for a in arrays]), 0, [])
    subtotal = taken_together(ravelled, axis)
    for a in arrays:
        finished.append(subtotal[at : at + a.size].reshape(a.shape))
        at += a.size
    return tuple(finished)


def sum_in_order(pieces, axes, order):
    lengths = [lax.axis_size(a) for a in axes]
    pieces = pieces.reshape(*lengths, *pieces.shape[1:])
    pieces = pieces.transpose(*order, *range(len(axes), pieces.ndim))
    pieces = pieces.reshape(-1, *pieces.shape[len(axes) :])
    for k in order:
        pieces = lax.psum_scatter(pieces, axes[k], scatter_dimension=0, tiled=True)
    return pieces[0]


def scatter_axes(array, axes, order, dim):
    peers = lax.axis_size(axes)
    return sum_in_order(in_blocks(array, dim, peers), axes, order)


def on_device(latent, hint, timestep, modulation, qkv_weight, out_weight, zero_weight, cotangent):
    tok, width = latent.shape
    heads_dev = width // HD
    scaling = HD ** (-0.5)
    control = lax.axis_index("group") == 0
    ctrl_mask = control.astype(jnp.float32)
    head_pos = lax.axis_index("head")
    steps_count = modulation.shape[1]
    pick = (lax.broadcasted_iota(jnp.int32, (steps_count,), 0) == timestep[0]).astype(jnp.float32)
    mods = jnp.sum(modulation[0] * pick[:, None, None], axis=0)
    shift, scale, gate = (mods[0], mods[1], mods[2])
    gate_dev = lax.dynamic_slice_in_dim(gate, head_pos * width, width, 0)
    scale_dev = lax.dynamic_slice_in_dim(scale, head_pos * width, width, 0)
    summed = (latent.astype(jnp.float32) + hint.astype(jnp.float32)).astype(jnp.bfloat16)
    inputs = jnp.where(control, summed, latent)
    whole = gather_directly(inputs, "head", 1)
    full_width = whole.shape[1]
    whole_f = whole.astype(jnp.float32)
    mean = jnp.mean(whole_f, axis=-1, keepdims=True)
    centred = whole_f - mean
    var = jnp.mean(centred * centred, axis=-1, keepdims=True)
    rstd = lax.rsqrt(var + EPS)
    nhat = centred * rstd
    normed = (nhat * (1.0 + scale) + shift).astype(jnp.bfloat16)
    w_qkv = qkv_weight[0]
    projected_qkv = jnp.einsum(
        "td,pde->pte", normed, w_qkv, preferred_element_type=jnp.float32
    ).astype(jnp.bfloat16)
    query, keys, values = (projected_qkv[0], projected_qkv[1], projected_qkv[2])
    q_heads = query.reshape(tok, heads_dev, HD)
    start_carry = (
        jnp.full((heads_dev, tok), -1e30, jnp.float32),
        jnp.zeros((heads_dev, tok), jnp.float32),
        jnp.zeros((tok, heads_dev, HD), jnp.float32),
    )

    def attend(carry, block):
        peak, total, acc = carry
        k_heads = block[0].reshape(-1, heads_dev, HD)
        v_heads = block[1].reshape(-1, heads_dev, HD)
        scores = (
            jnp.einsum("thd,shd->hts", q_heads, k_heads, preferred_element_type=jnp.float32)
            * scaling
        )
        new_peak = jnp.maximum(peak, jnp.max(scores, axis=-1))
        factor = jnp.exp(peak - new_peak)
        weights = jnp.exp(scores - new_peak[:, :, None])
        total = total * factor + jnp.sum(weights, axis=-1)
        acc = acc * factor.T[:, :, None] + jnp.einsum(
            "hts,shd->thd",
            weights.astype(jnp.bfloat16),
            v_heads,
            preferred_element_type=jnp.float32,
        )
        return ((new_peak, total, acc), None)

    kv_full = sent_together((keys, values), ROW, 0, 1)
    carry = start_carry
    key_rows = kv_full[0]
    rows = key_rows.shape[0]
    count = max(rows // tok, 1)
    size = rows // count
    blocks = (key_rows.reshape(count, size, width), kv_full[1].reshape(count, size, width))
    carry, unused = lax.scan(attend, carry, blocks)
    peak, total, acc = carry
    attn = (acc / total.T[:, :, None]).reshape(tok, width).astype(jnp.bfloat16)
    lse = peak + jnp.log(total)
    w_out = out_weight[0]
    branch_term = lax.dot_general(
        attn, w_out, (((1,), (1,)), ((), ())), preferred_element_type=jnp.float32
    )
    branch = sum_at_owner(branch_term, "head", 1)
    state = (inputs.astype(jnp.float32) + gate_dev * branch).astype(jnp.bfloat16)
    other_state = from_partner(state, "group", 0)
    control_out = jnp.where(control, state, other_state)
    main_out = jnp.where(control, other_state, state)
    hint_term = lax.dot_general(
        control_out, zero_weight, (((1,), (1,)), ((), ())), preferred_element_type=jnp.float32
    )
    projected = sum_at_owner(hint_term, "head", 1)
    mixed = (main_out.astype(jnp.float32) + projected).astype(jnp.bfloat16)
    cot_full = gather_directly(cotangent, "head", 1)
    hint_back = jnp.dot(cot_full, zero_weight, preferred_element_type=jnp.float32).astype(
        jnp.bfloat16
    )
    incoming = jnp.where(control, hint_back, cotangent)
    gated = (gate_dev * incoming.astype(jnp.float32)).astype(jnp.bfloat16)
    gated_full = gather_directly(gated, "head", 1)
    attn_grad = jnp.dot(gated_full, w_out, preferred_element_type=jnp.float32).astype(jnp.bfloat16)
    dsum = jnp.sum(
        (attn_grad.astype(jnp.float32) * attn.astype(jnp.float32)).reshape(tok, heads_dev, HD),
        axis=-1,
    )
    g_heads = attn_grad.reshape(tok, heads_dev, HD)
    full_keys, full_values = kv_full
    block_count = full_keys.shape[0] // tok
    key_blocks = (
        full_keys.reshape(block_count, tok, width),
        full_values.reshape(block_count, tok, width),
    )

    def backward_step(dq_acc, block):
        k_heads = block[0].reshape(tok, heads_dev, HD)
        v_heads = block[1].reshape(tok, heads_dev, HD)
        scores = (
            jnp.einsum("thd,shd->hts", q_heads, k_heads, preferred_element_type=jnp.float32)
            * scaling
        )
        probs = jnp.exp(scores - lse[:, :, None])
        dprobs = jnp.einsum("thd,shd->hts", g_heads, v_heads, preferred_element_type=jnp.float32)
        dscores = (probs * (dprobs - dsum.T[:, :, None])).astype(jnp.bfloat16)
        dq_acc = dq_acc + jnp.einsum(
            "hts,shd->thd", dscores, k_heads, preferred_element_type=jnp.float32
        )
        return (dq_acc, None)

    dq_acc, key_terms = lax.scan(
        backward_step, jnp.zeros((tok, heads_dev, HD), jnp.float32), key_blocks
    )
    dquery = (dq_acc * scaling).reshape(tok, width).astype(jnp.bfloat16)
    gathered = (
        lax.all_gather(query.astype(jnp.float32), ROW, axis=0, tiled=True).astype(query.dtype),
        lax.all_gather(attn_grad.astype(jnp.float32), ROW, axis=0, tiled=True).astype(
            attn_grad.dtype
        ),
        lax.all_gather(lse.T, ROW, axis=0, tiled=True),
        lax.all_gather(dsum, ROW, axis=0, tiled=True),
    )
    query_blocks = (
        gathered[0].reshape(block_count, tok, width),
        gathered[1].reshape(block_count, tok, width),
        gathered[2].reshape(block_count, tok, heads_dev),
        gathered[3].reshape(block_count, tok, heads_dev),
    )
    own_keys = keys.reshape(tok, heads_dev, HD)
    own_values = values.reshape(tok, heads_dev, HD)

    def owner_step(carry, block):
        dk_acc, dv_acc = carry
        qh = block[0].reshape(tok, heads_dev, HD)
        gh = block[1].reshape(tok, heads_dev, HD)
        scores = (
            jnp.einsum("thd,shd->hts", qh, own_keys, preferred_element_type=jnp.float32) * scaling
        )
        probs = jnp.exp(scores - block[2].T[:, :, None])
        dprobs = jnp.einsum("thd,shd->hts", gh, own_values, preferred_element_type=jnp.float32)
        dscores = (probs * (dprobs - block[3].T[:, :, None])).astype(jnp.bfloat16)
        dk_acc = dk_acc + jnp.einsum(
            "hts,thd->shd", dscores, qh, preferred_element_type=jnp.float32
        )
        dv_acc = dv_acc + jnp.einsum(
            "hts,thd->shd", probs.astype(jnp.bfloat16), gh, preferred_element_type=jnp.float32
        )
        return ((dk_acc, dv_acc), None)

    empty = jnp.zeros((tok, heads_dev, HD), jnp.float32)
    (dk_acc, dv_acc), unused = lax.scan(owner_step, (empty, empty), query_blocks)
    dkey_sum = (dk_acc * scaling).reshape(tok, width)
    dval_sum = dv_acc.reshape(tok, width)
    grads = jnp.stack([dquery, dkey_sum.astype(jnp.bfloat16), dval_sum.astype(jnp.bfloat16)])
    norm_term = jnp.einsum("pte,pde->td", grads, w_qkv, preferred_element_type=jnp.float32)
    nhat_dev = lax.dynamic_slice_in_dim(nhat, head_pos * width, width, 1)
    dnorm = sum_at_owner(norm_term, "head", 1)
    scaled = dnorm * (1.0 + scale_dev)
    first, second = together(
        (jnp.sum(scaled, axis=-1), jnp.sum(scaled * nhat_dev, axis=-1)), "head"
    )
    first = first[:, None] / full_width
    second = second[:, None] / full_width
    d_in = incoming.astype(jnp.float32) + rstd * (scaled - first - nhat_dev * second)
    half = tok // 2
    group_pos = lax.axis_index("group")
    own_half = lax.dynamic_slice_in_dim(d_in, group_pos * half, half, 0)
    sent_half = lax.dynamic_slice_in_dim(d_in, (1 - group_pos) * half, half, 0)
    other_half = from_partner(sent_half, "group", 0)
    latent_grad = (own_half + other_half)[None, None]
    hint_grad = jnp.where(control, own_half, other_half)[None, None]
    offset = group_pos * half
    cot_half = lax.dynamic_slice_in_dim(cot_full, offset, half, 0)
    control_half = lax.dynamic_slice_in_dim(control_out, offset, half, 0)
    columns = normed
    qkv_grad = scatter_axes(
        jnp.einsum("tc,pte->cpe", columns, grads, preferred_element_type=jnp.float32) * ctrl_mask,
        GROUP_ROW,
        (1, 0, 2),
        0,
    )
    columns = gated_full
    out_grad = lax.psum_scatter(
        lax.dot_general(columns, attn, (((0,), (0,)), ((), ())), preferred_element_type=jnp.float32)
        * ctrl_mask,
        GROUP_ROW,
        scatter_dimension=0,
        tiled=True,
    )
    columns = cot_half
    zero_grad = lax.psum_scatter(
        lax.dot_general(
            columns, control_half, (((0,), (0,)), ((), ())), preferred_element_type=jnp.float32
        ),
        GROUP_ROW,
        scatter_dimension=0,
        tiled=True,
    )
    return (mixed, latent_grad, hint_grad, qkv_grad, out_grad, zero_grad)


def solution(mesh):
    torus = Mesh(
        mesh.devices.reshape(mesh.shape["group"], 4, 2, mesh.shape["head"]),
        ("group", "row_0", "row_1", "head"),
    )
    return jax.shard_map(
        on_device,
        mesh=torus,
        in_specs=(
            P(ROW, "head"),
            P(ROW, "head"),
            P(),
            P("group", None, None, None),
            P("group", None, None, "head"),
            P("group", None, "head"),
            P(None, "head"),
            P(ROW, "head"),
        ),
        out_specs=(
            P(ROW, "head"),
            P(ROW, "group", None, "head"),
            P(ROW, "group", None, "head"),
            P(GROUP_ROW, None, "head"),
            P(GROUP_ROW, "head"),
            P(GROUP_ROW, "head"),
        ),
        check_vma=False,
    )
```

profile of v0, /device:TPU:1, one launch (start us, length us, event | category | flops | bytes accessed | tf_op | source)
XLA Modules:
  0.0 831.2 jit_solution(7527920485716257239)
XLA Ops:
  9.8 6.8 all-to-all-start
  18.1 19.2 %all-to-all-done = bf16[8,256,384]{2,1,0:T(8,128)(2,1)} async-done(((bf16[8,256,384]{2,1,0:T(8,128)(2,1)}), bf16[8,256,384]{2,1,0:T(8,128)(2,1)}, u32[]{:S(2)}, u32[]{:S(2)}) %all-to-all-start) | async-done | bytes 1572896 | tf_op jit(solution)/shard_map/all_to_all | solution.py:15
  52.2 59.9 %all-gather.5.cloned.1.call-done = bf16[2048,768]{1,0:T(8,128)(2,1)} async-done(((bf16[256,768]{1,0:T(8,128)(2,1)}), bf16[2048,768]{1,0:T(8,128)(2,1)}) %all-gather.5.cloned.1.call-update) | async-done | bytes 3145744 | tf_op jit(solution)/shard_map/all_gather | solution.py:31
  121.2 15.0 %while.39 = (s32[]{:T(128)}, f32[3,256]{1,0:T(4,128)S(1)}, f32[3,256]{1,0:T(4,128)S(1)}, f32[256,3,128]{0,2,1:T(8,128)S(1)}, bf16[8,256,384]{1,2,0:T(8,128)(2,1)...) while((s32[]{:T(128)}, f32[3,256]{1,0:T(4,128)S(1)}, ...), condition=%wide.region_6.7_spmd.clone, body=%wide.region_3.6_spmd.clone.sunk | while | flops 102142464 | bytes 4571253 | solution.py:152
  139.7 6.0 all-to-all-start.1
  145.8 37.4 %all-to-all-done.1 = f32[8,256,384]{2,1,0:T(8,128)} async-done(((f32[8,256,384]{2,1,0:T(8,128)}), f32[8,256,384]{2,1,0:T(8,128)}, u32[]{:S(2)}, u32[]{:S(2)}) %all-to-all-start.1) | async-done | bytes 3145760 | tf_op jit(solution)/shard_map/all_to_all | solution.py:46
  193.7 16.6 %all-to-all-done.3 = bf16[8,256,384]{1,2,0:T(8,128)(2,1)} async-done(((bf16[8,256,384]{1,2,0:T(8,128)(2,1)}), bf16[8,256,384]{1,2,0:T(8,128)(2,1)}, u32[]{:S(2)}, u32[]{:S(2)}) %all-to-all-start.3) | async-done | bytes 1572896 | tf_op jit(solution)/shard_map/all_to_all | solution.py:15
  240.3 29.6 %all_gather.17 = f32[2048,3]{0,1:T(4,128)} all-gather(f32[256,3]{0,1:T(4,128)S(1)} %bitcast.246), channel_id=1, replica_groups=mesh['group'=2,'row_0'=4,'row_1'=2,'head'=8] {'row_0','row_1'}, dimensions={0}, use_global_device_ids=true | all-gather | bytes 27648 | tf_op jit(solution)/shard_map/all_gather | solution.py:214
  275.7 15.6 %while.40 = (s32[]{:T(128)}, f32[256,3,128]{0,2,1:T(8,128)S(1)}, bf16[8,256,384]{1,2,0:T(8,128)(2,1)}, bf16[256,3,128]{2,0,1:T(8,128)(2,1)S(1)}, f32[3,256]{1,0:...) while((s32[]{:T(128)}, f32[256,3,128]{0,2,1:T(8,128)S(1)}, ...), condition=%wide.region_11.12_spmd.clone, body=%wide.region_10.11_spmd.clone.sunk | while | flops 152174592 | bytes 4135035 | solution.py:205
  291.6 28.0 %all_gather.19 = f32[2048,3]{0,1:T(4,128)S(1)} all-gather(f32[256,3]{0,1:T(4,128)S(1)} %get-tuple-element.758), channel_id=1, replica_groups=mesh['group'=2,'row_0'=4,'row_1'=2,'head'=8] {'row_0','row_1'}, dimensions={0}, use_global_device_ids=true | all-gather | bytes 27648 | tf_op jit(solution)/shard_map/all_gather | solution.py:215
  319.6 10.1 %all-gather.7.cloned.1.call-done = bf16[2048,384]{1,0:T(8,128)(2,1)} async-done(((bf16[256,384]{1,0:T(8,128)(2,1)}), bf16[2048,384]{1,0:T(8,128)(2,1)}) %all-gather.7.cloned.1.call-update) | async-done | bytes 1572880 | tf_op jit(solution)/shard_map/all_gather | solution.py:211
  329.7 25.7 %while.41 = (s32[]{:T(128)}, f32[256,3,128]{0,2,1:T(8,128)S(1)}, f32[256,3,128]{0,2,1:T(8,128)S(1)}, bf16[8,256,384]{2,1,0:T(8,128)(2,1)}, bf16[256,3,128]{2,0,1...) while((s32[]{:T(128)}, f32[256,3,128]{0,2,1:T(8,128)S(1)}, ...), condition=%wide.region_13.14_spmd.clone, body=%wide.region_12.13_spmd.clone.sunk | while | flops 202899456 | bytes 6703240 | solution.py:245
  355.9 9.3 %broadcast_multiply_fusion = f32[3072,3,384]{2,0,1:T(8,128)} fusion(f32[]{:T(128)S(6)} %convert_element_type.185, f32[256,3072]{1,0:T(8,128)} %subtract_multiply_fusion, f32[3072]{0:T(1024)S(1)} %bitcast.251, f32[3072]{0:T(1024)S(1)} %bitcast.250, bf16[1,256,384]{2,1,0:T(8,128)(2,1)S(1)} %copy.192, bf16[1,256,384]{2,1,0:T(8,128)(2,1)S(1)} %copy.191, ...), kind=kOutput, calls=%fused_computation.47 | convolution fusion | flops 1819607040 | bytes 17915908 | tf_op jit(solution)/shard_map/tc,pte->cpe/dot_general | solution.py:271
  365.1 11.7 %copy.197 = f32[4,2,2,192,3,384]{5,3,4,2,1,0:T(8,128)} copy(f32[4,2,2,192,3,384]{5,3,2,0,1,4:T(8,128)} %bitcast.215) | data formatting | bytes 28311552 | tf_op jit(solution)/shard_map/transpose | solution.py:77
  376.9 127.9 %reduce-scatter.6.cloned.1.call-done = f32[4,192,3,384]{3,1,2,0:T(8,128)} async-done(((f32[16,192,3,384]{3,1,2,0:T(8,128)}), f32[4,192,3,384]{3,1,2,0:T(8,128)}) %reduce-scatter.6.cloned.1.call-update) | async-done | bytes 3538960 | tf_op jit(solution)/shard_map/reduce_scatter | solution.py:80
  520.8 6.9 convolution_bitcast_fusion.3
  527.7 6.0 all-to-all-start.5
  536.5 34.7 %all-to-all-done.5 = f32[8,256,384]{2,1,0:T(8,128)} async-done(((f32[8,256,384]{2,1,0:T(8,128)}), f32[8,256,384]{2,1,0:T(8,128)}, u32[]{:S(2)}, u32[]{:S(2)}) %all-to-all-start.5) | async-done | bytes 3145760 | tf_op jit(solution)/shard_map/all_to_all | solution.py:46
  571.2 5.3 all-to-all-start.2
  581.2 32.9 %all-to-all-done.2 = f32[8,256,384]{2,1,0:T(8,128)} async-done(((f32[8,256,384]{2,1,0:T(8,128)}), f32[8,256,384]{2,1,0:T(8,128)}, u32[]{:S(2)}, u32[]{:S(2)}) %all-to-all-start.2) | async-done | bytes 3145760 | tf_op jit(solution)/shard_map/all_to_all | solution.py:46
  628.7 13.9 %collective-permute-done.1 = f32[128,384]{1,0:T(8,128)S(1)} collective-permute-done((f32[128,384]{1,0:T(8,128)S(1)}, f32[128,384]{1,0:T(8,128)S(1)}, u32[]{:S(2)}, u32[]{:S(2)}) %collective-permute-start.1) | collective-permute-done | bytes 196640 | tf_op jit(solution)/shard_map/ppermute | solution.py:57
  643.4 26.1 %reduce-scatter.14.cloned.1.call-done = f32[192,384]{1,0:T(8,128)} async-done(((f32[3072,384]{1,0:T(8,128)}), f32[192,384]{1,0:T(8,128)}) %reduce-scatter.14.cloned.1.call-update) | async-done | bytes 294928 | tf_op jit(solution)/shard_map/reduce_scatter | solution.py:285
  669.5 114.8 %reduce-scatter.12.cloned.1.call-done = f32[192,384]{1,0:T(8,128)} async-done(((f32[3072,384]{1,0:T(8,128)}), f32[192,384]{1,0:T(8,128)}) %reduce-scatter.12.cloned.1.call-update) | async-done | bytes 294928 | tf_op jit(solution)/shard_map/reduce_scatter | solution.py:277
  784.3 40.0 %reduce-scatter.10.cloned.1.call-done = f32[1,192,3,384]{3,1,2,0:T(8,128)} async-done(((f32[2,192,3,384]{3,1,2,0:T(8,128)}), f32[1,192,3,384]{3,1,2,0:T(8,128)}) %reduce-scatter.10.cloned.1.call-update) | async-done | bytes 884752 | tf_op jit(solution)/shard_map/reduce_scatter | solution.py:80
  (271 shorter events, 171.9 us)
Async XLA Ops:
  7.2 129.2 %copy-start = (bf16[1,3072,384]{2,1,0:T(8,128)(2,1)S(1)}, bf16[1,3072,384]{2,1,0:T(8,128)(2,1)}, u32[]{:S(2)}) copy-start(bf16[1,3072,384]{2,1,0:T(8,128)(2,1)} %param.19) | copy-start | bytes 7077892
  9.8 27.5 %all-to-all-start = ((bf16[8,256,384]{2,1,0:T(8,128)(2,1)}), bf16[8,256,384]{2,1,0:T(8,128)(2,1)}, u32[]{:S(2)}, u32[]{:S(2)}) async-start(bf16[8,256,384]{2,1,0:T(8,128)(2,1)} %broadcast_in_dim.24), calls=%async_computation | async-start | bytes 3145728 | tf_op jit(solution)/shard_map/all_to_all | solution.py:15
  16.6 95.5 %all-gather.5.cloned.1.call-start = ((), (), s32[]{:S(2)}) async-start(), calls=%async_computation.12 | async-start | bytes 3538944 | tf_op jit(solution)/shard_map/all_gather | solution.py:31
  42.4 192.0 %copy-start.17 = (f32[256]{0:T(256)}, f32[256]{0:T(256)S(1)}, u32[]{:S(2)}) copy-start(f32[256]{0:T(256)S(1)} %add_rsqrt_fusion) | copy-start | bytes 3076
  49.4 66.6 %copy-start.8 = (bf16[1,256,384]{2,1,0:T(8,128)(2,1)}, bf16[1,256,384]{2,1,0:T(8,128)(2,1)S(1)}, u32[]{:S(2)}) copy-start(bf16[1,256,384]{2,1,0:T(8,128)(2,1)S(1)} %get-tuple-element.437) | copy-start | bytes 589828
  139.7 43.5 %all-to-all-start.1 = ((f32[8,256,384]{2,1,0:T(8,128)}), f32[8,256,384]{2,1,0:T(8,128)}, u32[]{:S(2)}, u32[]{:S(2)}) async-start(f32[8,256,384]{2,1,0:T(8,128)} %convolution_bitcast_fusion.2), calls=%async_computation.1 | async-start | bytes 6291456 | tf_op jit(solution)/shard_map/all_to_all | solution.py:46
  184.5 25.9 %all-to-all-start.3 = ((bf16[8,256,384]{1,2,0:T(8,128)(2,1)}), bf16[8,256,384]{1,2,0:T(8,128)(2,1)}, u32[]{:S(2)}, u32[]{:S(2)}) async-start(bf16[8,256,384]{1,2,0:T(8,128)(2,1)} %broadcast_in_dim.25), calls=%async_computation.3 | async-start | bytes 3145728 | tf_op jit(solution)/shard_map/all_to_all | solution.py:15
  189.6 129.9 %all-gather.9.cloned.1.call-start = ((), (), s32[]{:S(2)}) async-start(), calls=%async_computation.19 | async-start | bytes 1769472 | tf_op jit(solution)/shard_map/all_gather | solution.py:210
  216.7 53.2 %all-to-all-start.4 = ((bf16[8,256,384]{1,2,0:T(8,128)(2,1)}), bf16[8,256,384]{1,2,0:T(8,128)(2,1)}, u32[]{:S(2)}, u32[]{:S(2)}) async-start(bf16[8,256,384]{1,2,0:T(8,128)(2,1)} %broadcast_in_dim.26), calls=%async_computation.4 | async-start | bytes 3145728 | tf_op jit(solution)/shard_map/all_to_all | solution.py:15
  221.8 107.8 %all-gather.7.cloned.1.call-start = ((), (), s32[]{:S(2)}) async-start(), calls=%async_computation.13 | async-start | bytes 1769472 | tf_op jit(solution)/shard_map/all_gather | solution.py:211
  275.5 229.3 %reduce-scatter.6.cloned.1.call-start = ((), (), s32[]{:S(2)}) async-start(), calls=%async_computation.14 | async-start | bytes 17694720 | tf_op jit(solution)/shard_map/reduce_scatter | solution.py:80
  275.7 54.0 %copy-start.3 = (f32[256,3,128]{0,2,1:T(8,128)S(1)}, f32[256,3,128]{0,2,1:T(8,128)}, u32[]{:S(2)}) copy-start(f32[256,3,128]{0,2,1:T(8,128)} %custom-call.5) | copy-start | bytes 1179652
  275.7 54.0 %copy-start.4 = (bf16[256,3,128]{2,0,1:T(8,128)(2,1)S(1)}, bf16[256,3,128]{2,0,1:T(8,128)(2,1)}, u32[]{:S(2)}) copy-start(bf16[256,3,128]{2,0,1:T(8,128)(2,1)} %copy.187) | copy-start | bytes 589828
  376.8 128.0 %copy-start.9 = (bf16[256,384]{1,0:T(8,128)(2,1)S(1)}, bf16[256,384]{1,0:T(8,128)(2,1)}, u32[]{:S(2)}) copy-start(bf16[256,384]{1,0:T(8,128)(2,1)} %get-tuple-element.447) | copy-start | bytes 589828
  376.8 199.7 %reduce-scatter.8.cloned.1.call-start = ((), (), s32[]{:S(2)}) async-start(), calls=%async_computation.15 | async-start | bytes 5308416 | tf_op jit(solution)/shard_map/reduce_scatter | solution.py:80
  504.8 164.7 %reduce-scatter.14.cloned.1.call-start = ((), (), s32[]{:S(2)}) async-start(), calls=%async_computation.18 | async-start | bytes 5013504 | tf_op jit(solution)/shard_map/reduce_scatter | solution.py:285
  504.9 5.8 collective-permute-start
  514.8 269.5 %reduce-scatter.12.cloned.1.call-start = ((), (), s32[]{:S(2)}) async-start(), calls=%async_computation.17 | async-start | bytes 5013504 | tf_op jit(solution)/shard_map/reduce_scatter | solution.py:277
  527.7 43.5 %all-to-all-start.5 = ((f32[8,256,384]{2,1,0:T(8,128)}), f32[8,256,384]{2,1,0:T(8,128)}, u32[]{:S(2)}, u32[]{:S(2)}) async-start(f32[8,256,384]{2,1,0:T(8,128)} %convolution_bitcast_fusion.3), calls=%async_computation.5 | async-start | bytes 6291456 | tf_op jit(solution)/shard_map/all_to_all | solution.py:46
  571.2 42.9 %all-to-all-start.2 = ((f32[8,256,384]{2,1,0:T(8,128)}), f32[8,256,384]{2,1,0:T(8,128)}, u32[]{:S(2)}, u32[]{:S(2)}) async-start(f32[8,256,384]{2,1,0:T(8,128)} %bitcast.227), calls=%async_computation.2 | async-start | bytes 6291456 | tf_op jit(solution)/shard_map/all_to_all | solution.py:46
  576.5 247.8 %reduce-scatter.10.cloned.1.call-start = ((), (), s32[]{:S(2)}) async-start(), calls=%async_computation.16 | async-start | bytes 2654208 | tf_op jit(solution)/shard_map/reduce_scatter | solution.py:80
  614.7 9.3 %all-to-all-start.6 = ((f32[8,1,512]{2,1,0:T(1,128)}), f32[8,1,512]{2,1,0:T(1,128)S(1)}, u32[]{:S(2)}, u32[]{:S(2)}) async-start(f32[8,1,512]{2,1,0:T(1,128)} %broadcast_in_dim.27), calls=%async_computation.6 | async-start | bytes 32768 | tf_op jit(solution)/shard_map/all_to_all | solution.py:15
  618.9 205.4 %copy-start.1 = (bf16[1,3072,384]{2,1,0:T(8,128)(2,1)S(1)}, bf16[1,3072,384]{2,1,0:T(8,128)(2,1)}, u32[]{:S(2)}) copy-start(bf16[1,3072,384]{2,1,0:T(8,128)(2,1)} %param.19) | copy-start | bytes 7077892
  626.7 16.0 %collective-permute-start.1 = (f32[128,384]{1,0:T(8,128)S(1)}, f32[128,384]{1,0:T(8,128)S(1)}, u32[]{:S(2)}, u32[]{:S(2)}) collective-permute-start(f32[128,384]{1,0:T(8,128)S(1)} %constant_dynamic-slice_fusion.6), channel_id=1, source_target_pairs={{0,64},{64,0},{1,65},{65,1},{2,66},{66,2},{3,67},{67,3},{4,68},{68... | collective-permute-start | bytes 589832 | tf_op jit(solution)/shard_map/ppermute | solution.py:57
  (11 other events, 130.8 us)
Sparse Core Ops, SparseCore 0:
  50.4 61.7 all-gather.4
  193.3 47.9 all-gather.8
  275.6 54.0 all-gather.6
  376.9 127.8 reduce-scatter.5
  507.0 49.9 reduce-scatter.7
  559.8 109.6 reduce-scatter.13
  672.5 111.8 reduce-scatter.11
  787.3 37.0 reduce-scatter.9
where the time goes:
time: 833 us; the launch traced here: 831 us
  waiting for transfers between devices  542 us (65%)
  local copies, waits for them, and re-layouts  83.4 us (10%)
  matrix products  62.3 us (7%)
  blocking collectives  57.6 us (7%)
  starting transfers between devices  41.3 us (5%)
  other arithmetic  28 us (3%)
  between operations  15.1 us (2%)
    reduce_scatter x3, waiting for transfers between devices, sum_in_order(): pieces = lax.psum_scatter(pieces, axes[k], scatter_dimension=0, tiled=True)  168 us
    reduce_scatter x1, waiting for transfers between devices, on_device(): lax.psum_scatter(lax.dot_general(columns, attn, (((0,), (0,)), ((), ())),...  115 us
    all_to_all x3, waiting for transfers between devices, sum_at_owner(): lax.all_to_all(pieces, axis, split_axis=0, concat_axis=0, tiled=True)  105 us
    all_gather x1, waiting for transfers between devices, sent_together(): lax.all_gather(both, axis, axis=dim, tiled=True)  59.9 us
    all_to_all x4, waiting for transfers between devices, copy_for_each(): return lax.all_to_all(copies, axis, split_axis=0, concat_axis=0, tiled=True)  38.6 us
    all_gather x1, blocking collectives, on_device(): lax.all_gather(lse.T, ROW, axis=0, tiled=True)  29.6 us
    all_gather x1, blocking collectives, on_device(): lax.all_gather(dsum, ROW, axis=0, tiled=True)  28 us
    dynamic_slice x40, local copies, waits for them, and re-layouts, on_device(): carry, unused = lax.scan(attend, carry, blocks)  27.8 us
  transfers between devices with their start and end apart: 17, of which 14 were waited for; matrix products, arithmetic and copies ran while one was open for 10% of the time, Pallas kernels for 0%

commit v1 on v0

--- a/solution.py
+++ b/solution.py
@@ -212,7 +212,7 @@
             attn_grad.dtype
         ),
         lax.all_gather(lse.T, ROW, axis=0, tiled=True),
-        lax.all_gather(dsum, ROW, axis=0, tiled=True),
+        jnp.concatenate(lax.all_to_all(jnp.stack([dsum] * lax.axis_size(ROW)), ROW, 0, 0), axis=0),
     )
     query_blocks = (
         gathered[0].reshape(block_count, tok, width),

time: 833 us -> 833 us (level)
  blocking collectives: 57.6 us -> 29.6 us
  waiting for transfers between devices: 542 us -> 565 us
    all_gather x1 -> x0, blocking collectives: 28 us -> none  [on_device(): lax.all_gather(dsum, ROW, axis=0, tiled=True)]
    all_gather x1, waiting for transfers between devices: 10.1 us -> 33.5 us  [on_device(): lax.all_gather(attn_grad.astype(jnp.float32), ROW, axis=0, tiled=True)]
  transfers between devices with their start and end apart: 17 -> 18, of which waited for: 14 -> 14; matrix products, arithmetic and copies ran while one was open for 10% -> 10% of each run, Pallas kernels for 0% -> 0%
where the time goes in v1:
time: 833 us; the launch traced here: 831 us
  waiting for transfers between devices  565 us (68%)
  local copies, waits for them, and re-layouts  84 us (10%)
  matrix products  62.3 us (7%)
  starting transfers between devices  45.2 us (5%)
  blocking collectives  29.6 us (4%)
  other arithmetic  28 us (3%)
  between operations  15.1 us (2%)
    reduce_scatter x3, waiting for transfers between devices, sum_in_order(): pieces = lax.psum_scatter(pieces, axes[k], scatter_dimension=0, tiled=True)  168 us
    reduce_scatter x1, waiting for transfers between devices, on_device(): lax.psum_scatter(lax.dot_general(columns, attn, (((0,), (0,)), ((), ())),...  114 us
    all_to_all x3, waiting for transfers between devices, sum_at_owner(): lax.all_to_all(pieces, axis, split_axis=0, concat_axis=0, tiled=True)  105 us
    all_gather x1, waiting for transfers between devices, sent_together(): lax.all_gather(both, axis, axis=dim, tiled=True)  59.9 us
    all_to_all x4, waiting for transfers between devices, copy_for_each(): return lax.all_to_all(copies, axis, split_axis=0, concat_axis=0, tiled=True)  38.6 us
    all_gather x1, waiting for transfers between devices, on_device(): lax.all_gather(attn_grad.astype(jnp.float32), ROW, axis=0, tiled=True)  33.5 us
    all_gather x1, blocking collectives, on_device(): lax.all_gather(lse.T, ROW, axis=0, tiled=True)  29.6 us
    dynamic_slice x40, local copies, waits for them, and re-layouts, on_device(): carry, unused = lax.scan(attend, carry, blocks)  27.7 us
  transfers between devices with their start and end apart: 18, of which 14 were waited for; matrix products, arithmetic and copies ran while one was open for 10% of the time, Pallas kernels for 0%

profile of v1, /device:TPU:1, one launch (start us, length us, event | category | flops | bytes accessed | tf_op | source)
XLA Modules:
  0.0 830.7 jit_solution(2184668806272117031)
XLA Ops:
  9.8 6.8 all-to-all-start
  18.1 19.2 %all-to-all-done = bf16[8,256,384]{2,1,0:T(8,128)(2,1)} async-done(((bf16[8,256,384]{2,1,0:T(8,128)(2,1)}), bf16[8,256,384]{2,1,0:T(8,128)(2,1)}, u32[]{:S(2)}, u32[]{:S(2)}) %all-to-all-start) | async-done | bytes 1572896 | tf_op jit(solution)/shard_map/all_to_all | solution.py:15
  43.4 5.3 fusion.37
  52.2 59.9 %all-gather.5.cloned.1.call-done = bf16[2048,768]{1,0:T(8,128)(2,1)} async-done(((bf16[256,768]{1,0:T(8,128)(2,1)}), bf16[2048,768]{1,0:T(8,128)(2,1)}) %all-gather.5.cloned.1.call-update) | async-done | bytes 3145744 | tf_op jit(solution)/shard_map/all_gather | solution.py:31
  121.2 15.0 %while.39 = (s32[]{:T(128)}, f32[3,256]{1,0:T(4,128)S(1)}, f32[3,256]{1,0:T(4,128)S(1)}, f32[256,3,128]{0,2,1:T(8,128)S(1)}, bf16[8,256,384]{1,2,0:T(8,128)(2,1)...) while((s32[]{:T(128)}, f32[3,256]{1,0:T(4,128)S(1)}, ...), condition=%wide.region_6.7_spmd.clone, body=%wide.region_3.6_spmd.clone.sunk | while | flops 102142464 | bytes 4571253 | solution.py:152
  139.7 6.0 all-to-all-start.1
  145.8 37.4 %all-to-all-done.1 = f32[8,256,384]{2,1,0:T(8,128)} async-done(((f32[8,256,384]{2,1,0:T(8,128)}), f32[8,256,384]{2,1,0:T(8,128)}, u32[]{:S(2)}, u32[]{:S(2)}) %all-to-all-start.1) | async-done | bytes 3145760 | tf_op jit(solution)/shard_map/all_to_all | solution.py:46
  193.7 16.6 %all-to-all-done.3 = bf16[8,256,384]{1,2,0:T(8,128)(2,1)} async-done(((bf16[8,256,384]{1,2,0:T(8,128)(2,1)}), bf16[8,256,384]{1,2,0:T(8,128)(2,1)}, u32[]{:S(2)}, u32[]{:S(2)}) %all-to-all-start.3) | async-done | bytes 1572896 | tf_op jit(solution)/shard_map/all_to_all | solution.py:15
  240.3 29.6 %all_gather.14 = f32[2048,3]{0,1:T(4,128)} all-gather(f32[256,3]{0,1:T(4,128)S(1)} %bitcast.245), channel_id=1, replica_groups=mesh['group'=2,'row_0'=4,'row_1'=2,'head'=8] {'row_0','row_1'}, dimensions={0}, use_global_device_ids=true | all-gather | bytes 27648 | tf_op jit(solution)/shard_map/all_gather | solution.py:214
  280.3 15.6 %while.40 = (s32[]{:T(128)}, f32[256,3,128]{0,2,1:T(8,128)S(1)}, bf16[8,256,384]{1,2,0:T(8,128)(2,1)}, bf16[256,3,128]{2,0,1:T(8,128)(2,1)S(1)}, f32[3,256]{1,0:...) while((s32[]{:T(128)}, f32[256,3,128]{0,2,1:T(8,128)S(1)}, ...), condition=%wide.region_11.12_spmd.clone, body=%wide.region_10.11_spmd.clone.sunk | while | flops 152174592 | bytes 4135035 | solution.py:205
  296.1 33.5 %all-gather.7.cloned.1.call-done = bf16[2048,384]{1,0:T(8,128)(2,1)} async-done(((bf16[256,384]{1,0:T(8,128)(2,1)}), bf16[2048,384]{1,0:T(8,128)(2,1)}) %all-gather.7.cloned.1.call-update) | async-done | bytes 1572880 | tf_op jit(solution)/shard_map/all_gather | solution.py:211
  329.6 25.8 %while.41 = (s32[]{:T(128)}, f32[256,3,128]{0,2,1:T(8,128)S(1)}, f32[256,3,128]{0,2,1:T(8,128)S(1)}, bf16[8,256,384]{2,1,0:T(8,128)(2,1)}, bf16[256,3,128]{2,0,1...) while((s32[]{:T(128)}, f32[256,3,128]{0,2,1:T(8,128)S(1)}, ...), condition=%wide.region_13.14_spmd.clone, body=%wide.region_12.13_spmd.clone.sunk | while | flops 202899456 | bytes 6703240 | solution.py:245
  355.9 9.3 %broadcast_multiply_fusion = f32[3072,3,384]{2,0,1:T(8,128)} fusion(f32[]{:T(128)S(6)} %convert_element_type.185, f32[256,3072]{1,0:T(8,128)} %subtract_multiply_fusion, f32[3072]{0:T(1024)S(1)} %bitcast.249, f32[3072]{0:T(1024)S(1)} %bitcast.248, bf16[1,256,384]{2,1,0:T(8,128)(2,1)S(1)} %copy.192, bf16[1,256,384]{2,1,0:T(8,128)(2,1)S(1)} %copy.191, ...), kind=kOutput, calls=%fused_computation.47 | convolution fusion | flops 1819607040 | bytes 17915908 | tf_op jit(solution)/shard_map/tc,pte->cpe/dot_general | solution.py:271
  365.2 11.7 %copy.197 = f32[4,2,2,192,3,384]{5,3,4,2,1,0:T(8,128)} copy(f32[4,2,2,192,3,384]{5,3,2,0,1,4:T(8,128)} %bitcast.214) | data formatting | bytes 28311552 | tf_op jit(solution)/shard_map/transpose | solution.py:77
  376.9 127.6 %reduce-scatter.6.cloned.1.call-done = f32[4,192,3,384]{3,1,2,0:T(8,128)} async-done(((f32[16,192,3,384]{3,1,2,0:T(8,128)}), f32[4,192,3,384]{3,1,2,0:T(8,128)}) %reduce-scatter.6.cloned.1.call-update) | async-done | bytes 3538960 | tf_op jit(solution)/shard_map/reduce_scatter | solution.py:80
  520.4 6.9 convolution_bitcast_fusion.3
  527.3 6.1 all-to-all-start.6
  536.3 34.7 %all-to-all-done.6 = f32[8,256,384]{2,1,0:T(8,128)} async-done(((f32[8,256,384]{2,1,0:T(8,128)}), f32[8,256,384]{2,1,0:T(8,128)}, u32[]{:S(2)}, u32[]{:S(2)}) %all-to-all-start.6) | async-done | bytes 3145760 | tf_op jit(solution)/shard_map/all_to_all | solution.py:46
  571.0 5.3 all-to-all-start.2
  581.0 32.9 %all-to-all-done.2 = f32[8,256,384]{2,1,0:T(8,128)} async-done(((f32[8,256,384]{2,1,0:T(8,128)}), f32[8,256,384]{2,1,0:T(8,128)}, u32[]{:S(2)}, u32[]{:S(2)}) %all-to-all-start.2) | async-done | bytes 3145760 | tf_op jit(solution)/shard_map/all_to_all | solution.py:46
  628.3 14.0 %collective-permute-done.1 = f32[128,384]{1,0:T(8,128)S(1)} collective-permute-done((f32[128,384]{1,0:T(8,128)S(1)}, f32[128,384]{1,0:T(8,128)S(1)}, u32[]{:S(2)}, u32[]{:S(2)}) %collective-permute-start.1) | collective-permute-done | bytes 196640 | tf_op jit(solution)/shard_map/ppermute | solution.py:57
  643.1 27.0 %reduce-scatter.14.cloned.1.call-done = f32[192,384]{1,0:T(8,128)} async-done(((f32[3072,384]{1,0:T(8,128)}), f32[192,384]{1,0:T(8,128)}) %reduce-scatter.14.cloned.1.call-update) | async-done | bytes 294928 | tf_op jit(solution)/shard_map/reduce_scatter | solution.py:285
  670.1 113.8 %reduce-scatter.12.cloned.1.call-done = f32[192,384]{1,0:T(8,128)} async-done(((f32[3072,384]{1,0:T(8,128)}), f32[192,384]{1,0:T(8,128)}) %reduce-scatter.12.cloned.1.call-update) | async-done | bytes 294928 | tf_op jit(solution)/shard_map/reduce_scatter | solution.py:277
  783.9 39.9 %reduce-scatter.10.cloned.1.call-done = f32[1,192,3,384]{3,1,2,0:T(8,128)} async-done(((f32[2,192,3,384]{3,1,2,0:T(8,128)}), f32[1,192,3,384]{3,1,2,0:T(8,128)}) %reduce-scatter.10.cloned.1.call-update) | async-done | bytes 884752 | tf_op jit(solution)/shard_map/reduce_scatter | solution.py:80
  (269 shorter events, 171.1 us)
Async XLA Ops:
  7.2 129.2 %copy-start = (bf16[1,3072,384]{2,1,0:T(8,128)(2,1)S(1)}, bf16[1,3072,384]{2,1,0:T(8,128)(2,1)}, u32[]{:S(2)}) copy-start(bf16[1,3072,384]{2,1,0:T(8,128)(2,1)} %param.19) | copy-start | bytes 7077892
  9.8 27.5 %all-to-all-start = ((bf16[8,256,384]{2,1,0:T(8,128)(2,1)}), bf16[8,256,384]{2,1,0:T(8,128)(2,1)}, u32[]{:S(2)}, u32[]{:S(2)}) async-start(bf16[8,256,384]{2,1,0:T(8,128)(2,1)} %broadcast_in_dim.24), calls=%async_computation | async-start | bytes 3145728 | tf_op jit(solution)/shard_map/all_to_all | solution.py:15
  16.6 95.5 %all-gather.5.cloned.1.call-start = ((), (), s32[]{:S(2)}) async-start(), calls=%async_computation.13 | async-start | bytes 3538944 | tf_op jit(solution)/shard_map/all_gather | solution.py:31
  42.4 192.0 %copy-start.15 = (f32[256]{0:T(256)}, f32[256]{0:T(256)S(1)}, u32[]{:S(2)}) copy-start(f32[256]{0:T(256)S(1)} %add_rsqrt_fusion) | copy-start | bytes 3076
  49.4 66.6 %copy-start.8 = (bf16[1,256,384]{2,1,0:T(8,128)(2,1)}, bf16[1,256,384]{2,1,0:T(8,128)(2,1)S(1)}, u32[]{:S(2)}) copy-start(bf16[1,256,384]{2,1,0:T(8,128)(2,1)S(1)} %get-tuple-element.437) | copy-start | bytes 589828
  139.7 43.5 %all-to-all-start.1 = ((f32[8,256,384]{2,1,0:T(8,128)}), f32[8,256,384]{2,1,0:T(8,128)}, u32[]{:S(2)}, u32[]{:S(2)}) async-start(f32[8,256,384]{2,1,0:T(8,128)} %convolution_bitcast_fusion.2), calls=%async_computation.1 | async-start | bytes 6291456 | tf_op jit(solution)/shard_map/all_to_all | solution.py:46
  184.5 25.9 %all-to-all-start.3 = ((bf16[8,256,384]{1,2,0:T(8,128)(2,1)}), bf16[8,256,384]{1,2,0:T(8,128)(2,1)}, u32[]{:S(2)}, u32[]{:S(2)}) async-start(bf16[8,256,384]{1,2,0:T(8,128)(2,1)} %broadcast_in_dim.25), calls=%async_computation.3 | async-start | bytes 3145728 | tf_op jit(solution)/shard_map/all_to_all | solution.py:15
  189.6 106.5 %all-gather.9.cloned.1.call-start = ((), (), s32[]{:S(2)}) async-start(), calls=%async_computation.20 | async-start | bytes 1769472 | tf_op jit(solution)/shard_map/all_gather | solution.py:210
  216.7 53.2 %all-to-all-start.4 = ((bf16[8,256,384]{1,2,0:T(8,128)(2,1)}), bf16[8,256,384]{1,2,0:T(8,128)(2,1)}, u32[]{:S(2)}, u32[]{:S(2)}) async-start(bf16[8,256,384]{1,2,0:T(8,128)(2,1)} %broadcast_in_dim.26), calls=%async_computation.4 | async-start | bytes 3145728 | tf_op jit(solution)/shard_map/all_to_all | solution.py:15
  221.8 107.8 %all-gather.7.cloned.1.call-start = ((), (), s32[]{:S(2)}) async-start(), calls=%async_computation.14 | async-start | bytes 1769472 | tf_op jit(solution)/shard_map/all_gather | solution.py:211
  276.1 20.1 %all-to-all-start.5 = ((f32[8,256,3]{1,2,0:T(4,128)}), f32[8,256,3]{1,2,0:T(4,128)}, u32[]{:S(2)}, u32[]{:S(2)}) async-start(f32[8,256,3]{1,2,0:T(4,128)} %stack.4), calls=%async_computation.5 | async-start | bytes 65536 | tf_op jit(solution)/shard_map/all_to_all | solution.py:215
  280.0 224.4 %reduce-scatter.6.cloned.1.call-start = ((), (), s32[]{:S(2)}) async-start(), calls=%async_computation.15 | async-start | bytes 17694720 | tf_op jit(solution)/shard_map/reduce_scatter | solution.py:80
  280.2 49.4 %copy-start.3 = (f32[256,3,128]{0,2,1:T(8,128)S(1)}, f32[256,3,128]{0,2,1:T(8,128)}, u32[]{:S(2)}) copy-start(f32[256,3,128]{0,2,1:T(8,128)} %custom-call.5) | copy-start | bytes 1179652
  376.8 127.7 %copy-start.9 = (bf16[256,384]{1,0:T(8,128)(2,1)S(1)}, bf16[256,384]{1,0:T(8,128)(2,1)}, u32[]{:S(2)}) copy-start(bf16[256,384]{1,0:T(8,128)(2,1)} %get-tuple-element.447) | copy-start | bytes 589828
  376.9 199.4 %reduce-scatter.8.cloned.1.call-start = ((), (), s32[]{:S(2)}) async-start(), calls=%async_computation.16 | async-start | bytes 5308416 | tf_op jit(solution)/shard_map/reduce_scatter | solution.py:80
  504.5 165.6 %reduce-scatter.14.cloned.1.call-start = ((), (), s32[]{:S(2)}) async-start(), calls=%async_computation.19 | async-start | bytes 5013504 | tf_op jit(solution)/shard_map/reduce_scatter | solution.py:285
  504.6 5.8 collective-permute-start
  514.5 269.5 %reduce-scatter.12.cloned.1.call-start = ((), (), s32[]{:S(2)}) async-start(), calls=%async_computation.18 | async-start | bytes 5013504 | tf_op jit(solution)/shard_map/reduce_scatter | solution.py:277
  527.3 43.7 %all-to-all-start.6 = ((f32[8,256,384]{2,1,0:T(8,128)}), f32[8,256,384]{2,1,0:T(8,128)}, u32[]{:S(2)}, u32[]{:S(2)}) async-start(f32[8,256,384]{2,1,0:T(8,128)} %convolution_bitcast_fusion.3), calls=%async_computation.6 | async-start | bytes 6291456 | tf_op jit(solution)/shard_map/all_to_all | solution.py:46
  571.0 42.9 %all-to-all-start.2 = ((f32[8,256,384]{2,1,0:T(8,128)}), f32[8,256,384]{2,1,0:T(8,128)}, u32[]{:S(2)}, u32[]{:S(2)}) async-start(f32[8,256,384]{2,1,0:T(8,128)} %bitcast.226), calls=%async_computation.2 | async-start | bytes 6291456 | tf_op jit(solution)/shard_map/all_to_all | solution.py:46
  576.3 247.6 %reduce-scatter.10.cloned.1.call-start = ((), (), s32[]{:S(2)}) async-start(), calls=%async_computation.17 | async-start | bytes 2654208 | tf_op jit(solution)/shard_map/reduce_scatter | solution.py:80
  614.5 9.3 %all-to-all-start.7 = ((f32[8,1,512]{2,1,0:T(1,128)}), f32[8,1,512]{2,1,0:T(1,128)S(1)}, u32[]{:S(2)}, u32[]{:S(2)}) async-start(f32[8,1,512]{2,1,0:T(1,128)} %broadcast_in_dim.27), calls=%async_computation.7 | async-start | bytes 32768 | tf_op jit(solution)/shard_map/all_to_all | solution.py:15
  618.7 205.2 %copy-start.1 = (bf16[1,3072,384]{2,1,0:T(8,128)(2,1)S(1)}, bf16[1,3072,384]{2,1,0:T(8,128)(2,1)}, u32[]{:S(2)}) copy-start(bf16[1,3072,384]{2,1,0:T(8,128)(2,1)} %param.19) | copy-start | bytes 7077892
  626.4 15.9 %collective-permute-start.1 = (f32[128,384]{1,0:T(8,128)S(1)}, f32[128,384]{1,0:T(8,128)S(1)}, u32[]{:S(2)}, u32[]{:S(2)}) collective-permute-start(f32[128,384]{1,0:T(8,128)S(1)} %constant_dynamic-slice_fusion.6), channel_id=1, source_target_pairs={{0,64},{64,0},{1,65},{65,1},{2,66},{66,2},{3,67},{67,3},{4,68},{68... | collective-permute-start | bytes 589832 | tf_op jit(solution)/shard_map/ppermute | solution.py:57
  (10 other events, 167.3 us)
Sparse Core Ops, SparseCore 0:
  50.4 61.7 all-gather.4
  193.3 47.9 all-gather.8
  275.6 53.9 all-gather.6
  377.0 127.4 reduce-scatter.5
  506.7 49.9 reduce-scatter.7
  559.5 110.5 reduce-scatter.13
  673.1 110.7 reduce-scatter.11
  786.9 36.9 reduce-scatter.9
